TPU v7x, 32 devices: a whole 2x2x4 slice. The times are simulated.
32 devices in a mesh: sub: 16 (over z, y, x), node: 2 (over core).
Axes of the slice: x: 2, y: 2, z: 4, core: 2. Of those that a mesh axis runs over, the one named last changes fastest.
Arguments:
- search_vectors: float32 [16384, 256], P('sub'), may hold values from -60 to 60
- ritz_values: float32 [256], replicated, may hold values from -0.9 to 0.9
- matrix_blocks: float32 [128, 4, 128, 128], P('sub'), may hold values from -0.25 to 0.25
- block_lists: int32 [128, 4], P('sub'), may hold values from 0 to 127, as said below
- inverses: float32 [4, 2, 128, 128, 128], P('node', None, 'sub'), may hold values from -0.5 to 0.5
- panels: float32 [16, 512, 1024], P('sub'), may hold values from -0.1875 to 0.1875
- separator_map: int32 [16, 4], P('sub'), may hold values from 0 to 7, as said below
- separator_shift: float32 [1024], replicated, may hold values from -0.9 to 0.9
Outputs:
- normalized_vectors: float32 [16384, 256], P('sub', 'node')
Inputs may be any that keep to these rules, and one draw needn't show every extreme that they name: `block_lists`: entry 0 of row g is g; the other entries of row g are distinct blocks from g - 4 to g + 4, none equal to g. `separator_map`: the entries of one row are distinct.
All inputs are finite; a program needn't handle non-finite values.
Results may differ from a plain program's by a relative error of at most 0.0001.
Values sent between devices are 32-bit elements; how exact they have to be, the bound alone decides.
A program may use at most 64 MiB of HBM per device.

v0:
```python
import math
import jax
import jax.numpy as jnp
from jax import lax
from jax.sharding import PartitionSpec as P

HALO_BLOCKS = 4
SEP_GROUPS = 8
HIGHEST = lax.Precision.HIGHEST


def with_halo(shard, sides, width):
    for axis, dim in sides:
        size, length = (lax.axis_size(axis), shard.shape[dim])
        up = [(i, (i + 1) % size) for i in range(size - 1)]
        down = [(j, i) for i, j in up]
        last = lax.slice_in_dim(shard, length - width, length, axis=dim)
        first = lax.slice_in_dim(shard, 0, width, axis=dim)
        before = lax.ppermute(last, axis, up)
        after = lax.ppermute(first, axis, down)
        shard = jnp.concatenate([before, shard, after], axis=dim)
    return shard


def scale_coarse(summed, shift_rows, real_shift, imag_shift):
    real_gap = real_shift[:, None, None] - shift_rows[None, :, None]
    imag_gap = imag_shift[:, None, None]
    modulus = real_gap * real_gap + imag_gap * imag_gap
    real_part = summed[:, 0]
    imag_part = summed[:, 1]
    return jnp.stack(
        [
            (real_part * real_gap + imag_part * imag_gap) / modulus,
            (imag_part * real_gap - real_part * imag_gap) / modulus,
        ],
        axis=1,
    )


def shards(
    search_vectors,
    ritz_values,
    matrix_blocks,
    block_lists,
    inverses,
    panels,
    separator_map,
    separator_shift,
):
    row_count, width = search_vectors.shape
    block_count, degree_count, block_size, _ = matrix_blocks.shape
    node_count = lax.axis_size("node")
    col_count = width // node_count
    node_index = lax.axis_index("node")
    sub_index = lax.axis_index("sub")
    column_start = node_index * col_count
    local_index = block_lists - sub_index * block_count + HALO_BLOCKS
    own_columns = lax.dynamic_slice_in_dim(search_vectors, column_start, col_count, 1)
    own_ritz = lax.dynamic_slice_in_dim(ritz_values, column_start, col_count, 0)
    padded = with_halo(own_columns, (("sub", 0),), HALO_BLOCKS * block_size)
    picked = padded.reshape(block_count + 2 * HALO_BLOCKS, block_size, -1)[local_index]
    local_part = (
        jnp.einsum("bkij,bkjm->bim", matrix_blocks, picked, precision=HIGHEST).reshape(
            row_count, -1
        )
        - own_columns * own_ritz[None, :]
    )
    residual = lax.all_gather(local_part, "node", axis=1, tiled=True)
    node_local = inverses.shape[0]
    total_nodes = node_local * node_count
    node_ids = (node_index * node_local + jnp.arange(node_local, dtype=jnp.int32)).astype(
        jnp.float32
    )
    angles = math.pi * (node_ids + 0.5) / total_nodes
    real_shift = jnp.cos(angles)
    imag_shift = jnp.sin(angles)
    res_blocks = residual.reshape(block_count, block_size, width)
    first_guess = jnp.einsum("ncbij,bjm->ncbim", inverses, res_blocks, precision=HIGHEST).reshape(
        node_local, 2, row_count, width
    )
    my_panel = panels[0]
    sep_count = my_panel.shape[0] // block_size
    partial_value = jnp.einsum("sr,ncrm->ncsm", my_panel, first_guess, precision=HIGHEST)
    one_hot = (
        separator_map[0][:, None] == jnp.arange(SEP_GROUPS, dtype=jnp.int32)[None, :]
    ).astype(jnp.float32)
    spread = jnp.einsum(
        "pg,ncpkm->ncgkm",
        one_hot,
        partial_value.reshape(node_local, 2, sep_count, block_size, width),
        precision=HIGHEST,
    ).reshape(node_local, 2, SEP_GROUPS * block_size, width)
    summed_all = lax.psum(spread, "sub")
    scaled = scale_coarse(summed_all, separator_shift, real_shift, imag_shift)
    picked_back = jnp.einsum(
        "pg,ncgkm->ncpkm",
        one_hot,
        scaled.reshape(node_local, 2, SEP_GROUPS, block_size, width),
        precision=HIGHEST,
    ).reshape(node_local, 2, sep_count * block_size, width)
    spread_back = jnp.einsum("sr,ncsm->ncrm", my_panel, picked_back, precision=HIGHEST).reshape(
        node_local, 2, block_count, block_size, width
    )
    products = jnp.einsum("ncbij,ndbjm->ncdbim", inverses, spread_back, precision=HIGHEST).reshape(
        node_local, 2, 2, row_count, width
    )
    sol_real = first_guess[:, 0] - (products[:, 0, 0] - products[:, 1, 1])
    sol_imag = first_guess[:, 1] - (products[:, 0, 1] + products[:, 1, 0])
    weight_real = 2.0 / total_nodes * real_shift
    weight_imag = 2.0 / total_nodes * imag_shift
    weighted = jnp.sum(
        weight_real[:, None, None] * sol_real - weight_imag[:, None, None] * sol_imag, axis=0
    )
    node_total = lax.psum_scatter(weighted, "node", scatter_dimension=1, tiled=True)
    updated = lax.dynamic_slice_in_dim(search_vectors, column_start, col_count, 1) - node_total
    squares = lax.psum(jnp.sum(updated * updated, axis=0), "sub")
    total_rows = row_count * lax.axis_size("sub")
    return updated * lax.rsqrt(squares / total_rows + 1e-06)[None, :]


def solution(mesh):
    return jax.shard_map(
        shards,
        mesh=mesh,
        in_specs=(
            P("sub", None),
            P(),
            P("sub", None, None, None),
            P("sub", None),
            P("node", None, "sub", None, None),
            P("sub", None, None),
            P("sub", None),
            P(),
        ),
        out_specs=P("sub", "node"),
        check_vma=False,
    )
```

profile of v0, /device:TPU:0, one launch (start us, length us, event | category | flops | bytes accessed | tf_op | source)
XLA Modules:
  0.0 344.4 jit_solution(13921328892674392484)
XLA Ops:
  7.8 4.9 %collective-permute-start = (f32[512,128]{1,0:T(8,128)S(1)}, f32[512,128]{1,0:T(8,128)S(1)}, u32[]{:S(2)}, u32[]{:S(2)}) collective-permute-start(f32[512,128]{1,0:T(8,128)S(1)} %get-tuple-element.9), channel_id=1, source_target_pairs={{0,2},{2,4},{4,6},{6,8},{8,10},{10,12},{12,14},{14,16},{16,18},{18... | collective-permute-start | bytes 786440 | tf_op jit(solution)/shard_map/ppermute | solution.py:19
  16.6 7.2 %collective-permute-done = f32[512,128]{1,0:T(8,128)S(1)} collective-permute-done((f32[512,128]{1,0:T(8,128)S(1)}, f32[512,128]{1,0:T(8,128)S(1)}, u32[]{:S(2)}, u32[]{:S(2)}) %collective-permute-start) | collective-permute-done | bytes 262176 | tf_op jit(solution)/shard_map/ppermute | solution.py:19
  23.8 2.0 collective-permute-done.1
  26.9 2.0 gather_fusion
  28.9 4.7 %fusion.41 = f32[8,128,128,1]{1,2,3,0:T(8,128)S(1)} fusion(f32[8,4,128,128]{3,2,1,0:T(8,128)} %bitcast.141, f32[8,4,128,128]{3,2,1,0:T(8,128)} %param.10), kind=kOutput, calls=%fused_computation.59 | convolution fusion | flops 805306368 | bytes 4718592 | tf_op jit(solution)/shard_map/bkij,bkjm->bim/dot_general | solution.py:63
  34.7 9.0 %all-gather.2.cloned.1.call-done = f32[1024,256]{1,0:T(8,128)} async-done(((f32[1024,128]{1,0:T(8,128)}), f32[1024,256]{1,0:T(8,128)}) %all-gather.2.cloned.1.call-update) | async-done | bytes 1048592 | tf_op jit(solution)/shard_map/all_gather | solution.py:68
  43.7 4.7 %convolution_bitcast_fusion.1 = f32[2,2,8,128,256]{4,3,1,0,2:T(8,128)S(1)} fusion(f32[8,128,256,1,1]{2,1,4,3,0:T(8,128)} %bitcast.145, f32[2,2,8,128,128]{4,3,2,1,0:T(8,128)S(1)} %copy-done), kind=kOutput, calls=%fused_computation.9 | convolution fusion | flops 1610612736 | bytes 7340032 | tf_op jit(solution)/shard_map/ncbij,bjm->ncbim/dot_general | solution.py:78
  48.9 2.0 copy-done.1
  50.9 14.7 %fusion.25 = f32[2,2,512,256]{2,3,1,0:T(8,128)} fusion(f32[2,2,1024,256]{3,2,1,0:T(8,128)S(1)} %bitcast.134, f32[1,512,1024]{2,1,0:T(8,128)S(1)} %copy-done.3), kind=kOutput, calls=%fused_computation.34 | convolution fusion | flops 6442450944 | bytes 8388608 | tf_op jit(solution)/shard_map/sr,ncrm->ncsm/dot_general | solution.py:83
  65.6 2.9 reshape.134
  68.5 4.1 %copy.20 = f32[2,2,4,128,256]{4,2,3,1,0:T(4,128)} copy(f32[2,2,4,128,256]{3,2,4,1,0:T(4,128)} %reshape.134) | data formatting | bytes 4194304 | tf_op jit(solution)/shard_map/reshape | solution.py:90
  72.6 3.8 %convolution_bitcast_fusion = f32[2,2,8,128,256]{4,2,3,1,0:T(8,128)S(1)} fusion(f32[2,2,4,128,256]{4,2,3,1,0:T(4,128)} %copy.20, s32[4]{0:T(128)S(1)} %bitcast.146), kind=kOutput, calls=%fused_computation.8 | convolution fusion | flops 50331680 | bytes 6291472 | tf_op jit(solution)/shard_map/pg,ncpkm->ncgkm/dot_general | solution.py:87
  76.4 3.3 copy.21
  80.4 169.0 %all-reduce.2.cloned.1.call-done = f32[2,2,1024,256]{3,2,1,0:T(8,128)} async-done(((f32[2,2,1024,256]{3,2,1,0:T(8,128)}), f32[2,2,1024,256]{3,2,1,0:T(8,128)}) %all-reduce.2.cloned.1.call-update) | async-done | bytes 4194320 | tf_op jit(solution)/shard_map/psum | solution.py:93
  249.4 3.0 add_divide_fusion
  254.8 2.1 fusion.28
  258.5 7.0 %fusion.19 = f32[2,2,256,1024]{3,2,1,0:T(8,128)S(1)} fusion(f32[2,2,512,256]{3,2,1,0:T(8,128)S(1)} %bitcast.144, f32[1,512,1024]{2,1,0:T(8,128)S(1)} %copy-done.4), kind=kOutput, calls=%fused_computation.26 | convolution fusion | flops 6442450944 | bytes 8388608 | tf_op jit(solution)/shard_map/sr,ncsm->ncrm/dot_general | solution.py:101
  266.7 7.8 %fusion.6 = f32[2,2,2,8,128,256]{5,4,1,2,3,0:T(8,128)S(1)} fusion(f32[2,2,8,128,256,1]{3,2,4,1,0,5:T(8,128)S(1)} %bitcast.137, f32[2,2,8,128,128]{4,3,2,1,0:T(8,128)S(1)} %copy-done), kind=kOutput, calls=%fused_computation.7 | convolution fusion | flops 3221225472 | bytes 14680064 | tf_op jit(solution)/shard_map/ncbij,ndbjm->ncdbim/dot_general | solution.py:104
  274.5 4.2 %copy.28 = f32[2,2,2,8,128,256]{5,4,3,2,1,0:T(8,128)} copy(f32[2,2,2,8,128,256]{5,4,1,2,3,0:T(8,128)S(1)} %fusion.6) | data formatting | bytes 16777216 | tf_op jit(solution)/shard_map/ncbij,ndbjm->ncdbim/transpose | solution.py:104
  278.7 5.6 %fusion.14 = f32[1024,256]{1,0:T(8,128)} fusion(f32[2,2,2,1024,256]{4,3,2,1,0:T(8,128)} %bitcast.136, f32[2,2,1024,256]{3,2,1,0:T(8,128)S(1)} %bitcast.135, f32[2]{0:T(128)S(1)} %get-tuple-element.13, f32[2]{0:T(128)S(1)} %get-tuple-element.14), kind=kLoop, calls=%fused_computation.16 | loop fusion | flops 3932160 | bytes 13631504 | tf_op jit(solution)/shard_map/reduce_sum | solution.py:111
  284.3 7.6 %reduce-scatter.2.cloned.1.call-done = f32[1024,128]{1,0:T(8,128)} async-done(((f32[1024,256]{1,0:T(8,128)}), f32[1024,128]{1,0:T(8,128)}) %reduce-scatter.2.cloned.1.call-update) | async-done | bytes 524304 | tf_op jit(solution)/shard_map/reduce_scatter | solution.py:114
  291.9 1.9 multiply_reduce_fusion
  293.8 42.0 %psum.15 = f32[128]{0:T(128)S(1)} all-reduce(f32[128]{0:T(128)S(1)} %get-tuple-element.5), channel_id=1, replica_groups=mesh['sub'=16,'node'=2] {'sub'}, use_global_device_ids=true, to_apply=%region_4.0 | all-reduce | flops 128 | bytes 1024 | tf_op jit(solution)/shard_map/psum | solution.py:116
  335.8 1.9 broadcast_multiply_fusion
  (41 shorter events, 13.7 us)
Async XLA Ops:
  6.5 37.2 %copy-start = (f32[2,2,8,128,128]{4,3,2,1,0:T(8,128)S(1)}, f32[2,2,8,128,128]{4,3,2,1,0:T(8,128)}, u32[]{:S(2)}) copy-start(f32[2,2,8,128,128]{4,3,2,1,0:T(8,128)} %param.12) | copy-start | bytes 6291460
  6.5 37.2 %all-gather.2.cloned.1.call-start = ((), (), s32[]{:S(2)}) async-start(), calls=%async_computation.1 | async-start | bytes 1572864 | tf_op jit(solution)/shard_map/all_gather | solution.py:68
  7.8 16.1 %collective-permute-start = (f32[512,128]{1,0:T(8,128)S(1)}, f32[512,128]{1,0:T(8,128)S(1)}, u32[]{:S(2)}, u32[]{:S(2)}) collective-permute-start(f32[512,128]{1,0:T(8,128)S(1)} %get-tuple-element.9), channel_id=1, source_target_pairs={{0,2},{2,4},{4,6},{6,8},{8,10},{10,12},{12,14},{14,16},{16,18},{18... | collective-permute-start | bytes 786440 | tf_op jit(solution)/shard_map/ppermute | solution.py:19
  12.7 13.2 %collective-permute-start.1 = (f32[512,128]{1,0:T(8,128)S(1)}, f32[512,128]{1,0:T(8,128)}, u32[]{:S(2)}, u32[]{:S(2)}) collective-permute-start(f32[512,128]{1,0:T(8,128)S(1)} %get-tuple-element.10), channel_id=1, source_target_pairs={{2,0},{4,2},{6,4},{8,6},{10,8},{12,10},{14,12},{16,14},{18,16},{20... | collective-permute-start | bytes 786440 | tf_op jit(solution)/shard_map/ppermute | solution.py:20
  28.9 4.7 %copy-start.5 = (f32[1024,256]{1,0:T(8,128)S(1)}, f32[1024,256]{1,0:T(8,128)}, u32[]{:S(2)}) copy-start(f32[1024,256]{1,0:T(8,128)} %param.8) | copy-start | bytes 3145732
  34.5 214.9 %all-reduce.2.cloned.1.call-start = ((), (), s32[]{:S(2)}) async-start(), calls=%async_computation.2 | async-start | bytes 8388608 | tf_op jit(solution)/shard_map/psum | solution.py:93
  48.5 2.4 copy-start.3
  48.9 2.0 copy-start.1
  68.5 4.1 %copy-start.7 = (s32[1,4]{1,0:T(1,128)S(1)}, s32[1,4]{1,0:T(1,128)}, u32[]{:S(2)}) copy-start(s32[1,4]{1,0:T(1,128)} %param.14) | copy-start | bytes 52
  79.7 0.7 copy-start.6
  79.7 212.2 %reduce-scatter.2.cloned.1.call-start = ((), (), s32[]{:S(2)}) async-start(), calls=%async_computation.3 | async-start | bytes 1572864 | tf_op jit(solution)/shard_map/reduce_scatter | solution.py:114
  256.9 1.6 copy-start.4
  274.5 4.2 %copy-start.2 = (f32[2,2,8,128,256]{4,3,2,1,0:T(8,128)S(1)}, f32[2,2,8,128,256]{4,3,2,1,0:T(8,128)}, u32[]{:S(2)}) copy-start(f32[2,2,8,128,256]{4,3,2,1,0:T(8,128)} %copy-done.1) | copy-start | bytes 12582916
Sparse Core Ops, SparseCore 0:
  34.6 9.0 all-gather.1
  79.8 169.5 all-reduce.1
  284.4 7.4 reduce-scatter.1
where the time goes:
time: 348 us; the launch traced here: 344 us
  waiting for transfers between devices  195 us (56%)
  matrix products  44.8 us (13%)
  blocking collectives  42 us (12%)
  local copies, waits for them, and re-layouts  27.8 us (8%)
  other arithmetic  15.1 us (4%)
  between operations  13.5 us (4%)
  starting transfers between devices  6.44 us (2%)
    psum x1, waiting for transfers between devices, shards(): summed_all = lax.psum(spread, 'sub')  169 us
    psum x1, blocking collectives, shards(): squares = lax.psum(jnp.sum(updated * updated, axis=0), 'sub')  42 us
    dot_general x1, matrix products, shards(): jnp.einsum('sr,ncrm->ncsm', my_panel, first_guess, precision=HIGHEST)  14.7 us
    all_gather x1, waiting for transfers between devices, shards(): residual = lax.all_gather(local_part, 'node', axis=1, tiled=True)  9.01 us
    dot_general x1, matrix products, shards(): jnp.einsum('ncbij,ndbjm->ncdbim', inverses, spread_back, precision=HIGHEST)  7.8 us
    reduce_scatter x1, waiting for transfers between devices, shards(): lax.psum_scatter(weighted, 'node', scatter_dimension=1, tiled=True)  7.57 us
    ppermute x1, waiting for transfers between devices, with_halo(): before = lax.ppermute(last, axis, up)  7.18 us
    reshape x2, local copies, waits for them, and re-layouts, shards(): partial_value.reshape(node_local, 2, sep_count, block_size, width)  7.06 us
  transfers between devices with their start and end apart: 5, of which 5 were waited for; matrix products, arithmetic and copies ran while one was open for 1% of the time, Pallas kernels for 0%

commit v1 on v0

--- a/solution.py
+++ b/solution.py
@@ -90,7 +90,15 @@
         partial_value.reshape(node_local, 2, sep_count, block_size, width),
         precision=HIGHEST,
     ).reshape(node_local, 2, SEP_GROUPS * block_size, width)
-    summed_all = lax.psum(spread, "sub")
+
+    def scan_goods(vec):
+        w1 = vec
+        n_shards = lax.axis_size("sub")
+        for dd in [src_i for src_i in (1, 2, 4, 8, 16) if src_i < n_shards]:
+            w1 = w1 + lax.ppermute(w1, "sub", [(nth, nth ^ dd) for nth in range(n_shards)])
+        return w1
+
+    summed_all = scan_goods(spread)
     scaled = scale_coarse(summed_all, separator_shift, real_shift, imag_shift)
     picked_back = jnp.einsum(
         "pg,ncgkm->ncpkm",

time: 348 us -> 642 us (1.84)
  waiting for transfers between devices: 195 us -> 477 us
  starting transfers between devices: 6.44 us -> 14.5 us
    ppermute x0 -> x4, waiting for transfers between devices: none -> 449 us  [scan_goods(): lax.ppermute(w1, 'sub', [(nth, nth ^ dd) for nth in range(n_shards)])]
    psum x1 -> x0, waiting for transfers between devices: 169 us -> none  [shards(): summed_all = lax.psum(spread, 'sub')]
    add x0 -> x4, other arithmetic: none -> 8.11 us  [scan_goods(): w1 + lax.ppermute(w1, 'sub', [(nth, nth ^ dd) for nth in range(n_shards)])]
    ppermute x0 -> x4, starting transfers between devices: none -> 8.08 us  [scan_goods(): lax.ppermute(w1, 'sub', [(nth, nth ^ dd) for nth in range(n_shards)])]
  transfers between devices with their start and end apart: 5 -> 8, of which waited for: 5 -> 8; matrix products, arithmetic and copies ran while one was open for 1% -> 0% of each run, Pallas kernels for 0% -> 0%
where the time goes in v1:
time: 642 us; the launch traced here: 639 us
  waiting for transfers between devices  477 us (74%)
  matrix products  45 us (7%)
  blocking collectives  41.9 us (7%)
  local copies, waits for them, and re-layouts  25.4 us (4%)
  other arithmetic  21.2 us (3%)
  starting transfers between devices  14.5 us (2%)
  between operations  13.8 us (2%)
    ppermute x4, waiting for transfers between devices, scan_goods(): lax.ppermute(w1, 'sub', [(nth, nth ^ dd) for nth in range(n_shards)])  449 us
    psum x1, blocking collectives, shards(): squares = lax.psum(jnp.sum(updated * updated, axis=0), 'sub')  41.9 us
    dot_general x1, matrix products, shards(): jnp.einsum('sr,ncrm->ncsm', my_panel, first_guess, precision=HIGHEST)  14.9 us
  transfers between devices with their start and end apart: 8, of which 8 were waited for; matrix products, arithmetic and copies ran while one was open for 0% of the time, Pallas kernels for 0%

profile of v1, /device:TPU:0, one launch (start us, length us, event | category | flops | bytes accessed | tf_op | source)
XLA Modules:
  0.0 638.6 jit_solution(4236765382701957985)
XLA Ops:
  7.8 4.9 collective-permute-start
  16.6 7.2 %collective-permute-done = f32[512,128]{1,0:T(8,128)S(1)} collective-permute-done((f32[512,128]{1,0:T(8,128)S(1)}, f32[512,128]{1,0:T(8,128)S(1)}, u32[]{:S(2)}, u32[]{:S(2)}) %collective-permute-start) | collective-permute-done | bytes 262176 | tf_op jit(solution)/shard_map/ppermute | solution.py:19
  26.9 2.0 gather_fusion
  28.9 4.7 fusion.41
  34.7 9.0 %all-gather.2.cloned.1.call-done = f32[1024,256]{1,0:T(8,128)} async-done(((f32[1024,128]{1,0:T(8,128)}), f32[1024,256]{1,0:T(8,128)}) %all-gather.2.cloned.1.call-update) | async-done | bytes 1048592 | tf_op jit(solution)/shard_map/all_gather | solution.py:68
  43.7 4.7 convolution_bitcast_fusion.1
  50.9 14.9 %fusion.25 = f32[2,2,512,256]{2,3,1,0:T(8,128)} fusion(f32[2,2,1024,256]{3,2,1,0:T(8,128)S(1)} %bitcast.135, f32[1,512,1024]{2,1,0:T(8,128)S(1)} %copy-done.3), kind=kOutput, calls=%fused_computation.34 | convolution fusion | flops 6442450944 | bytes 8388608 | tf_op jit(solution)/shard_map/sr,ncrm->ncsm/dot_general | solution.py:83
  65.8 2.9 reshape.134
  68.7 4.1 copy.20
  72.8 3.8 convolution_bitcast_fusion
  79.7 91.0 %collective-permute-done.2 = f32[2,2,1024,256]{3,2,1,0:T(8,128)S(1)} collective-permute-done((f32[2,2,1024,256]{3,2,1,0:T(8,128)S(1)}, f32[2,2,1024,256]{3,2,1,0:T(8,128)S(1)}, u32[]{:S(2)}, u32[]{:S(2)}) %collective-permute-start.2) | collective-permute-done | bytes 4194336 | tf_op jit(solution)/shard_map/ppermute | solution.py:98
  173.6 90.2 %collective-permute-done.3 = f32[2,2,1024,256]{3,2,1,0:T(8,128)S(1)} collective-permute-done((f32[2,2,1024,256]{3,2,1,0:T(8,128)S(1)}, f32[2,2,1024,256]{3,2,1,0:T(8,128)S(1)}, u32[]{:S(2)}, u32[]{:S(2)}) %collective-permute-start.3) | collective-permute-done | bytes 4194336 | tf_op jit(solution)/shard_map/ppermute | solution.py:98
  266.1 89.3 %collective-permute-done.4 = f32[2,2,1024,256]{3,2,1,0:T(8,128)S(1)} collective-permute-done((f32[2,2,1024,256]{3,2,1,0:T(8,128)S(1)}, f32[2,2,1024,256]{3,2,1,0:T(8,128)S(1)}, u32[]{:S(2)}, u32[]{:S(2)}) %collective-permute-start.4) | collective-permute-done | bytes 4194336 | tf_op jit(solution)/shard_map/ppermute | solution.py:98
  355.4 2.5 add.115
  357.9 2.6 collective-permute-start.5
  360.8 178.4 %collective-permute-done.5 = f32[2,2,1024,256]{3,2,1,0:T(8,128)} collective-permute-done((f32[2,2,1024,256]{3,2,1,0:T(8,128)}, f32[2,2,1024,256]{3,2,1,0:T(8,128)}, u32[]{:S(2)}, u32[]{:S(2)}) %collective-permute-start.5) | collective-permute-done | bytes 4194336 | tf_op jit(solution)/shard_map/ppermute | solution.py:98
  539.2 4.0 add.116
  546.6 2.1 fusion.28
  550.3 7.0 %fusion.19 = f32[2,2,256,1024]{3,2,1,0:T(8,128)S(1)} fusion(f32[2,2,512,256]{3,2,1,0:T(8,128)S(1)} %bitcast.145, f32[1,512,1024]{2,1,0:T(8,128)S(1)} %copy-done.4), kind=kOutput, calls=%fused_computation.26 | convolution fusion | flops 6442450944 | bytes 8388608 | tf_op jit(solution)/shard_map/sr,ncsm->ncrm/dot_general | solution.py:109
  558.6 7.8 %fusion.6 = f32[2,2,2,8,128,256]{5,4,1,2,3,0:T(8,128)S(1)} fusion(f32[2,2,8,128,256,1]{3,2,4,1,0,5:T(8,128)S(1)} %bitcast.139, f32[2,2,8,128,128]{4,3,2,1,0:T(8,128)S(1)} %copy-done), kind=kOutput, calls=%fused_computation.7 | convolution fusion | flops 3221225472 | bytes 14680064 | tf_op jit(solution)/shard_map/ncbij,ndbjm->ncdbim/dot_general | solution.py:112
  566.4 4.2 copy.28
  570.5 5.6 fusion.14
  576.1 9.6 %reduce-scatter.2.cloned.1.call-done = f32[1024,128]{1,0:T(8,128)} async-done(((f32[1024,256]{1,0:T(8,128)}), f32[1024,128]{1,0:T(8,128)}) %reduce-scatter.2.cloned.1.call-update) | async-done | bytes 524304 | tf_op jit(solution)/shard_map/reduce_scatter | solution.py:122
  587.7 41.9 %psum.7 = f32[128]{0:T(128)S(1)} all-reduce(f32[128]{0:T(128)S(1)} %get-tuple-element.5), channel_id=1, replica_groups=mesh['sub'=16,'node'=2] {'sub'}, use_global_device_ids=true, to_apply=%region_3.0 | all-reduce | flops 128 | bytes 1024 | tf_op jit(solution)/shard_map/psum | solution.py:124
  (50 shorter events, 30.3 us)
Async XLA Ops:
  6.5 37.2 %copy-start = (f32[2,2,8,128,128]{4,3,2,1,0:T(8,128)S(1)}, f32[2,2,8,128,128]{4,3,2,1,0:T(8,128)}, u32[]{:S(2)}) copy-start(f32[2,2,8,128,128]{4,3,2,1,0:T(8,128)} %param.12) | copy-start | bytes 6291460
  6.5 37.2 %all-gather.2.cloned.1.call-start = ((), (), s32[]{:S(2)}) async-start(), calls=%async_computation.1 | async-start | bytes 1572864 | tf_op jit(solution)/shard_map/all_gather | solution.py:68
  7.8 16.1 %collective-permute-start = (f32[512,128]{1,0:T(8,128)S(1)}, f32[512,128]{1,0:T(8,128)S(1)}, u32[]{:S(2)}, u32[]{:S(2)}) collective-permute-start(f32[512,128]{1,0:T(8,128)S(1)} %get-tuple-element.9), channel_id=1, source_target_pairs={{0,2},{2,4},{4,6},{6,8},{8,10},{10,12},{12,14},{14,16},{16,18},{18... | collective-permute-start | bytes 786440 | tf_op jit(solution)/shard_map/ppermute | solution.py:19
  12.7 13.2 %collective-permute-start.1 = (f32[512,128]{1,0:T(8,128)S(1)}, f32[512,128]{1,0:T(8,128)}, u32[]{:S(2)}, u32[]{:S(2)}) collective-permute-start(f32[512,128]{1,0:T(8,128)S(1)} %get-tuple-element.10), channel_id=1, source_target_pairs={{2,0},{4,2},{6,4},{8,6},{10,8},{12,10},{14,12},{16,14},{18,16},{20... | collective-permute-start | bytes 786440 | tf_op jit(solution)/shard_map/ppermute | solution.py:20
  28.9 4.7 copy-start.5
  34.5 551.3 %reduce-scatter.2.cloned.1.call-start = ((), (), s32[]{:S(2)}) async-start(), calls=%async_computation.2 | async-start | bytes 1572864 | tf_op jit(solution)/shard_map/reduce_scatter | solution.py:122
  48.5 2.4 copy-start.3
  48.9 2.0 copy-start.1
  68.7 4.1 copy-start.7
  77.9 92.8 %collective-permute-start.2 = (f32[2,2,1024,256]{3,2,1,0:T(8,128)S(1)}, f32[2,2,1024,256]{3,2,1,0:T(8,128)S(1)}, u32[]{:S(2)}, u32[]{:S(2)}) collective-permute-start(f32[2,2,1024,256]{3,2,1,0:T(8,128)S(1)} %bitcast.138), channel_id=1, source_target_pairs={{0,2},{2,0},{4,6},{6,4},{8,10},{10,8},{12,14},{14,12},{16,18},{18,... | collective-permute-start | bytes 12582920 | tf_op jit(solution)/shard_map/ppermute | solution.py:98
  171.8 92.0 %collective-permute-start.3 = (f32[2,2,1024,256]{3,2,1,0:T(8,128)S(1)}, f32[2,2,1024,256]{3,2,1,0:T(8,128)S(1)}, u32[]{:S(2)}, u32[]{:S(2)}) collective-permute-start(f32[2,2,1024,256]{3,2,1,0:T(8,128)S(1)} %bitcast_add_fusion), channel_id=1, source_target_pairs={{0,4},{2,6},{4,0},{6,2},{8,12},{10,14},{12,8},{14,10},{16,20},{18,... | collective-permute-start | bytes 12582920 | tf_op jit(solution)/shard_map/ppermute | solution.py:98
  264.3 96.4 %copy-start.6 = (f32[1024]{0:T(1024)S(1)}, f32[1024]{0:T(1024)}, u32[]{:S(2)}) copy-start(f32[1024]{0:T(1024)} %param.15) | copy-start | bytes 12292
  264.3 91.1 %collective-permute-start.4 = (f32[2,2,1024,256]{3,2,1,0:T(8,128)S(1)}, f32[2,2,1024,256]{3,2,1,0:T(8,128)S(1)}, u32[]{:S(2)}, u32[]{:S(2)}) collective-permute-start(f32[2,2,1024,256]{3,2,1,0:T(8,128)S(1)} %add.114), channel_id=1, source_target_pairs={{0,8},{2,10},{4,12},{6,14},{8,0},{10,2},{12,4},{14,6},{16,24},{18,... | collective-permute-start | bytes 12582920 | tf_op jit(solution)/shard_map/ppermute | solution.py:98
  357.9 181.3 %collective-permute-start.5 = (f32[2,2,1024,256]{3,2,1,0:T(8,128)}, f32[2,2,1024,256]{3,2,1,0:T(8,128)}, u32[]{:S(2)}, u32[]{:S(2)}) collective-permute-start(f32[2,2,1024,256]{3,2,1,0:T(8,128)} %add.115), channel_id=1, source_target_pairs={{0,16},{2,18},{4,20},{6,22},{8,24},{10,26},{12,28},{14,30},{16,0},... | collective-permute-start | bytes 12582920 | tf_op jit(solution)/shard_map/ppermute | solution.py:98
  548.7 1.6 copy-start.4
  566.4 4.2 copy-start.2
Sparse Core Ops, SparseCore 0:
  34.6 9.0 all-gather.1
  576.3 9.4 reduce-scatter.1
